TPU v7x, 32 devices: a whole 2x2x4 slice. The times are simulated.
32 devices in a mesh: rep: 16 (over z, y, core), shard: 2 (over x).
Axes of the slice: x: 2, y: 2, z: 4, core: 2. Of those that a mesh axis runs over, the one named last changes fastest.
Arguments:
- tokens: bfloat16 [4096, 1024], P(('rep', 'shard')), may hold values from -6 to 6
- positions: int32 [4096], P(('rep', 'shard')), may hold values from 0 to 381, as said below
- routes: int32 [4096, 2], P(('rep', 'shard')), may hold values from 0 to 7, all different within a row; in each aligned block of 128 rows (0 to 127, 128 to 255, ...) at most 48 rows name the same one
- gates: float32 [4096, 2], P(('rep', 'shard')), may hold values from 0.1 to 1
- cotangent: bfloat16 [4096, 1024], P(('rep', 'shard')), may hold values from -6 to 6
- attn_gain: bfloat16 [1024], P('shard'), may hold values from 0.5 to 1.5
- w_query: bfloat16 [1024, 1024], P('shard'), may hold values from -0.75 to 0.75
- key_weight: bfloat16 [1024, 512], P('shard'), may hold values from -0.75 to 0.75
- value_weight: bfloat16 [1024, 512], P('shard'), may hold values from -0.1875 to 0.1875
- w_out: bfloat16 [1024, 1024], P('shard'), may hold values from -3 to 3
- ffn_gain: bfloat16 [1024], P('shard'), may hold values from 0.5 to 1.5
- w_gate_up: bfloat16 [8, 1024, 1024], P('shard'), may hold values from -0.1875 to 0.1875
- w_down: bfloat16 [8, 512, 1024], P('shard'), may hold values from -1.5 to 1.5
Outputs:
- output: bfloat16 [4096, 1024], P(('rep', 'shard'))
- input_grad: bfloat16 [4096, 1024], P(('rep', 'shard'))
- grad_attn_gain: float32 [1024], P('shard')
- grad_w_query: float32 [1024, 1024], P('shard')
- grad_w_key: float32 [1024, 512], P('shard')
- grad_w_value: float32 [1024, 512], P('shard')
- grad_w_out: float32 [1024, 1024], P('shard')
- grad_ffn_gain: float32 [1024], P('shard')
- grad_w_gate_up: float32 [8, 1024, 1024], P('shard')
- grad_w_down: float32 [8, 512, 1024], P('shard')
Inputs may be any that keep to these rules, and one draw needn't show every extreme that they name: Within each sequence of 128 tokens positions start at 0 and rise by 1, 2 or 3 from token to token; in one sequence they rise by 3 at every token. `routes`: among the rows of one device no expert is named more than 48 times.
All inputs are finite; a program needn't handle non-finite values.
Results may differ from a plain program's by a relative error of at most 0.023.
Values may be sent and summed in bfloat16 or wider, within the bound.
No kernel may reach another device: no remote copies, remote signals or barrier semaphores. Data moves between devices by JAX's collectives and lax.ppermute only.
A program may use at most 192 MiB of HBM per device.

v0:
```python
import jax
import jax.numpy as jnp
from jax import lax
from jax.sharding import PartitionSpec as P

QUERY_HEADS = 16
KEY_VALUE_HEADS = 8
HEAD_DIM = 64
F = 512
EXPERTS = 8
TOP = 2
CAP = 48


RMS_EPS = 1e-06
RES_MULT = 0.22
ATT_MULT = 0.015625
ROPE_BASE = 10000.0


def rms_norm(values, norm_gain):
    inverse = lax.rsqrt(jnp.mean(values * values, axis=-1, keepdims=True) + RMS_EPS)
    return values * inverse * norm_gain


def rope_tables(positions):
    half_dim = HEAD_DIM // 2
    frequency = ROPE_BASE ** (-(2.0 * jnp.arange(half_dim, dtype=jnp.float32)) / HEAD_DIM)
    angles = positions.astype(jnp.float32)[:, None] * frequency[None, :]
    return (jnp.cos(angles)[:, None, :], jnp.sin(angles)[:, None, :])


def apply_rotary(values, cosine_table, sinusoid_table):
    half_dim = values.shape[-1] // 2
    front_half = values[..., :half_dim]
    back_half = values[..., half_dim:]
    return jnp.concatenate(
        [
            front_half * cosine_table - back_half * sinusoid_table,
            back_half * cosine_table + front_half * sinusoid_table,
        ],
        axis=-1,
    )


def swiglu(gate_up):
    return jax.nn.silu(gate_up[..., :F]) * gate_up[..., F:]


def slot_table(routes):
    flat_routes = routes.reshape(-1)
    onehot = (flat_routes[:, None] == jnp.arange(EXPERTS, dtype=jnp.int32)[None, :]).astype(
        jnp.int32
    )
    before = jnp.cumsum(onehot, axis=0) - onehot
    ranked = jnp.sum(before * onehot, axis=1)
    slot_index = flat_routes * CAP + ranked
    owners = jnp.arange(flat_routes.shape[0], dtype=jnp.int32) // TOP
    sources = jnp.zeros((EXPERTS * CAP,), jnp.int32).at[slot_index].set(owners)
    filled = jnp.zeros((EXPERTS * CAP,), jnp.float32).at[slot_index].set(1.0)
    return (slot_index, sources, filled)


def masked_scores(query_head_rows, key_head_rows, causal):
    scores = ATT_MULT * jnp.einsum(
        "qhgd,khd->hgqk", query_head_rows, key_head_rows, preferred_element_type=jnp.float32
    )
    return jnp.where(causal, scores, -1e30)


def per_device(
    tokens,
    positions,
    routes,
    gates,
    cotangent,
    attn_gain,
    w_query,
    key_weight,
    value_weight,
    w_out,
    ffn_gain,
    w_gate_up,
    w_down,
):
    sequence_length = tokens.shape[0]
    model_width = tokens.shape[1]
    heads_per_group = QUERY_HEADS // KEY_VALUE_HEADS
    cosine_table, sinusoid_table = rope_tables(positions)
    causal = jnp.arange(sequence_length)[:, None] >= jnp.arange(sequence_length)[None, :]
    gain_one, full_query, full_key, full_value, full_out, gain_two = (
        lax.all_gather(attn_gain, "shard", axis=0, tiled=True),
        lax.all_gather(w_query, "shard", axis=0, tiled=True),
        lax.all_gather(key_weight, "shard", axis=0, tiled=True),
        lax.all_gather(value_weight, "shard", axis=0, tiled=True),
        lax.all_gather(w_out, "shard", axis=0, tiled=True),
        lax.all_gather(ffn_gain, "shard", axis=0, tiled=True),
    )
    inputs = tokens.astype(jnp.float32)
    normalized_input, norm_pull = jax.vjp(rms_norm, inputs, gain_one.astype(jnp.float32))
    normed_low = normalized_input.astype(jnp.bfloat16)
    query_proj = jnp.dot(normed_low, full_query, preferred_element_type=jnp.float32).reshape(
        sequence_length, QUERY_HEADS, HEAD_DIM
    )
    key_proj = jnp.dot(normed_low, full_key, preferred_element_type=jnp.float32).reshape(
        sequence_length, KEY_VALUE_HEADS, HEAD_DIM
    )
    value_head_rows = (
        jnp.dot(normed_low, full_value, preferred_element_type=jnp.float32)
        .astype(jnp.bfloat16)
        .reshape(sequence_length, KEY_VALUE_HEADS, HEAD_DIM)
    )
    query_head_rows = (
        apply_rotary(query_proj, cosine_table, sinusoid_table)
        .astype(jnp.bfloat16)
        .reshape(sequence_length, KEY_VALUE_HEADS, heads_per_group, HEAD_DIM)
    )
    key_head_rows = apply_rotary(key_proj, cosine_table, sinusoid_table).astype(jnp.bfloat16)
    scores = masked_scores(query_head_rows, key_head_rows, causal)
    top_score = jnp.max(scores, axis=-1, keepdims=True)
    log_total = top_score + jnp.log(jnp.sum(jnp.exp(scores - top_score), axis=-1, keepdims=True))
    probs_low = jnp.exp(scores - log_total).astype(jnp.bfloat16)
    attended = jnp.einsum(
        "hgqk,khd->qhgd", probs_low, value_head_rows, preferred_element_type=jnp.float32
    )
    attended = attended.reshape(sequence_length, QUERY_HEADS * HEAD_DIM).astype(jnp.bfloat16)
    branch = jnp.dot(attended, full_out, preferred_element_type=jnp.float32)
    hidden = inputs + RES_MULT * branch
    second, second_pull = jax.vjp(rms_norm, hidden, gain_two.astype(jnp.float32))
    second_low = second.astype(jnp.bfloat16)
    slot_index, sources, filled = slot_table(routes)
    dispatched = (second_low[sources] * filled[:, None].astype(jnp.bfloat16)).reshape(
        EXPERTS, CAP, model_width
    )
    received = lax.all_to_all(dispatched, "shard", split_axis=0, concat_axis=1, tiled=True)
    gate_up = jnp.einsum("ecd,edf->ecf", received, w_gate_up, preferred_element_type=jnp.float32)
    activated, act_pull = jax.vjp(swiglu, gate_up)
    act_low = activated.astype(jnp.bfloat16)
    expert_out = jnp.einsum(
        "ecf,efd->ecd", act_low, w_down, preferred_element_type=jnp.float32
    ).astype(jnp.bfloat16)
    returned = lax.all_to_all(expert_out, "shard", split_axis=1, concat_axis=0, tiled=True).reshape(
        EXPERTS * CAP, model_width
    )
    picked = returned[slot_index].reshape(sequence_length, TOP, model_width).astype(jnp.float32)
    combined = jnp.sum(gates[:, :, None] * picked, axis=1)
    output = (hidden + RES_MULT * combined).astype(jnp.bfloat16)
    upstream = cotangent.astype(jnp.float32)
    route_grad = (gates[:, :, None] * (RES_MULT * upstream)[:, None, :]).astype(jnp.bfloat16)
    route_grad = route_grad.reshape(sequence_length * TOP, model_width)
    out_grad = jnp.zeros((EXPERTS * CAP, model_width), jnp.bfloat16).at[slot_index].set(route_grad)
    out_grad = out_grad.reshape(EXPERTS, CAP, model_width)
    grad_arrived = lax.all_to_all(out_grad, "shard", split_axis=0, concat_axis=1, tiled=True)
    outbound_grad = jnp.einsum(
        "ecf,ecd->efd", act_low, grad_arrived, preferred_element_type=jnp.float32
    )
    act_grad = jnp.einsum("ecd,efd->ecf", grad_arrived, w_down, preferred_element_type=jnp.float32)
    inner_grad = act_pull(act_grad)[0].astype(jnp.bfloat16)
    inbound_grad = jnp.einsum(
        "ecd,ecf->edf", received, inner_grad, preferred_element_type=jnp.float32
    )
    rows_grad = jnp.einsum(
        "ecf,edf->ecd", inner_grad, w_gate_up, preferred_element_type=jnp.float32
    ).astype(jnp.bfloat16)
    rows_back = lax.all_to_all(rows_grad, "shard", split_axis=1, concat_axis=0, tiled=True).reshape(
        EXPERTS * CAP, model_width
    )
    second_grad = jnp.sum(
        rows_back[slot_index].reshape(sequence_length, TOP, model_width).astype(jnp.float32), axis=1
    )
    hidden_part, grad_latter = second_pull(second_grad)
    hidden_grad = upstream + hidden_part
    full_query, full_key, full_value, full_out = (
        lax.all_gather(w_query, "shard", axis=0, tiled=True),
        lax.all_gather(key_weight, "shard", axis=0, tiled=True),
        lax.all_gather(value_weight, "shard", axis=0, tiled=True),
        lax.all_gather(w_out, "shard", axis=0, tiled=True),
    )
    branch_grad = (RES_MULT * hidden_grad).astype(jnp.bfloat16)
    attended_gradient = jnp.dot(branch_grad, full_out.T, preferred_element_type=jnp.float32).astype(
        jnp.bfloat16
    )
    attended_gradient = attended_gradient.reshape(
        sequence_length, KEY_VALUE_HEADS, heads_per_group, HEAD_DIM
    )
    rescored = masked_scores(query_head_rows, key_head_rows, causal)
    probs = jnp.exp(rescored - log_total)
    probs_again = probs.astype(jnp.bfloat16)
    probs_grad = jnp.einsum(
        "qhgd,khd->hgqk", attended_gradient, value_head_rows, preferred_element_type=jnp.float32
    )
    row_inner = jnp.sum(probs * probs_grad, axis=-1, keepdims=True)
    score_grad = (probs * (probs_grad - row_inner)).astype(jnp.bfloat16)
    value_gradient = jnp.einsum(
        "hgqk,qhgd->khd", probs_again, attended_gradient, preferred_element_type=jnp.float32
    )
    value_gradient = value_gradient.astype(jnp.bfloat16).reshape(
        sequence_length, KEY_VALUE_HEADS * HEAD_DIM
    )
    query_turned = ATT_MULT * jnp.einsum(
        "hgqk,khd->qhgd", score_grad, key_head_rows, preferred_element_type=jnp.float32
    )
    rotated_keys = ATT_MULT * jnp.einsum(
        "hgqk,qhgd->khd", score_grad, query_head_rows, preferred_element_type=jnp.float32
    )
    query_grad = (
        apply_rotary(
            query_turned.reshape(sequence_length, QUERY_HEADS, HEAD_DIM),
            cosine_table,
            -sinusoid_table,
        )
        .astype(jnp.bfloat16)
        .reshape(sequence_length, QUERY_HEADS * HEAD_DIM)
    )
    key_grad = (
        apply_rotary(rotated_keys, cosine_table, -sinusoid_table)
        .astype(jnp.bfloat16)
        .reshape(sequence_length, KEY_VALUE_HEADS * HEAD_DIM)
    )
    normed_grad = jnp.dot(query_grad, full_query.T, preferred_element_type=jnp.float32)
    normed_grad = normed_grad + jnp.dot(key_grad, full_key.T, preferred_element_type=jnp.float32)
    normed_grad = normed_grad + jnp.dot(
        value_gradient, full_value.T, preferred_element_type=jnp.float32
    )
    input_part, grad_former = norm_pull(normed_grad)
    input_grad = (hidden_grad + input_part).astype(jnp.bfloat16)
    projected = jnp.concatenate([query_grad, key_grad, value_gradient], axis=1)
    proj_grad = jnp.dot(attended.T, branch_grad, preferred_element_type=jnp.float32)
    proj_owned = lax.psum_scatter(
        jnp.dot(normed_low.T, projected, preferred_element_type=jnp.float32).astype(jnp.bfloat16),
        "shard",
        scatter_dimension=0,
        tiled=True,
    ).astype(jnp.float32)
    owned_out, owned_former, owned_latter = (
        lax.psum_scatter(
            proj_grad.astype(jnp.bfloat16), "shard", scatter_dimension=0, tiled=True
        ).astype(jnp.float32),
        lax.psum_scatter(
            grad_former.astype(jnp.bfloat16), "shard", scatter_dimension=0, tiled=True
        ).astype(jnp.float32),
        lax.psum_scatter(
            grad_latter.astype(jnp.bfloat16), "shard", scatter_dimension=0, tiled=True
        ).astype(jnp.float32),
    )
    query_cols = QUERY_HEADS * HEAD_DIM
    key_columns = KEY_VALUE_HEADS * HEAD_DIM
    owned_query = proj_owned[:, :query_cols]
    owned_key = proj_owned[:, query_cols : query_cols + key_columns]
    owned_value = proj_owned[:, query_cols + key_columns :]
    (
        summed_former,
        summed_query,
        summed_key,
        summed_value,
        summed_out,
        summed_latter,
        summed_inbound,
        summed_outbound,
    ) = (
        lax.psum(owned_former.astype(jnp.bfloat16), "rep").astype(jnp.float32),
        lax.psum(owned_query.astype(jnp.bfloat16), "rep").astype(jnp.float32),
        lax.psum(owned_key.astype(jnp.bfloat16), "rep").astype(jnp.float32),
        lax.psum(owned_value.astype(jnp.bfloat16), "rep").astype(jnp.float32),
        lax.psum(owned_out.astype(jnp.bfloat16), "rep").astype(jnp.float32),
        lax.psum(owned_latter.astype(jnp.bfloat16), "rep").astype(jnp.float32),
        lax.psum(inbound_grad.astype(jnp.bfloat16), "rep").astype(jnp.float32),
        lax.psum(outbound_grad.astype(jnp.bfloat16), "rep").astype(jnp.float32),
    )
    return (
        output,
        input_grad,
        summed_former,
        summed_query,
        summed_key,
        summed_value,
        summed_out,
        summed_latter,
        summed_inbound,
        summed_outbound,
    )


def solution(mesh):
    in_specs = (
        P(("rep", "shard"), None),
        P(("rep", "shard")),
        P(("rep", "shard"), None),
        P(("rep", "shard"), None),
        P(("rep", "shard"), None),
        P("shard"),
        P("shard", None),
        P("shard", None),
        P("shard", None),
        P("shard", None),
        P("shard"),
        P("shard", None, None),
        P("shard", None, None),
    )
    out_specs = (
        P(("rep", "shard"), None),
        P(("rep", "shard"), None),
        P("shard"),
        P("shard", None),
        P("shard", None),
        P("shard", None),
        P("shard", None),
        P("shard"),
        P("shard", None, None),
        P("shard", None, None),
    )
    return jax.shard_map(
        per_device, mesh=mesh, in_specs=in_specs, out_specs=out_specs, check_vma=False
    )
```

profile of v0, /device:TPU:0, one launch (start us, length us, event | category | flops | bytes accessed | tf_op | source)
XLA Modules:
  0.0 622.7 jit_solution(14890413966478427559)
XLA Ops:
  8.0 0.7 all-gather.9.cloned.1.call-update
  11.4 0.7 mul.421
  12.9 2.7 scatter_custom_fusion.2
  15.5 4.2 all-to-all-start.2
  20.4 20.1 %all-gather = bf16[2,1,512]{2,1,0:T(2,128)(2,1)S(1)} all-gather(bf16[1,1,512]{2,1,0:T(2,128)(2,1)S(1)} %reshape.313), channel_id=1, replica_groups=mesh['rep'=16,'shard'=2] {'shard'}, dimensions={0}, use_global_device_ids=true | all-gather | bytes 3072 | tf_op jit(solution)/shard_map/all_gather | solution.py:92
  41.3 4.4 all-gather.1
  45.7 1.4 scatter_custom_fusion
  47.1 1.4 scatter_custom_fusion.1
  48.6 0.8 fusion.32
  49.4 1.6 convolution_convert_fusion.8
  51.2 13.8 %all-gather.9.cloned.1.call-done = bf16[1024,512]{1,0:T(8,128)(2,1)} async-done(((bf16[512,512]{1,0:T(8,128)(2,1)}), bf16[1024,512]{1,0:T(8,128)(2,1)}) %all-gather.9.cloned.1.call-update) | async-done | bytes 1048592 | tf_op jit(solution)/shard_map/all_gather | solution.py:94
  64.9 1.8 fusion.50
  66.8 32.8 %all-gather.11.cloned.1.call-done = bf16[1024,1024]{1,0:T(8,128)(2,1)} async-done(((bf16[512,1024]{1,0:T(8,128)(2,1)}), bf16[1024,1024]{1,0:T(8,128)(2,1)}) %all-gather.11.cloned.1.call-update) | async-done | bytes 2097168 | tf_op jit(solution)/shard_map/all_gather | solution.py:93
  99.6 2.6 fusion.48
  103.3 30.8 %all-gather.13.cloned.1.call-done = bf16[1024,1024]{1,0:T(8,128)(2,1)} async-done(((bf16[512,1024]{1,0:T(8,128)(2,1)}), bf16[1024,1024]{1,0:T(8,128)(2,1)}) %all-gather.13.cloned.1.call-update) | async-done | bytes 2097168 | tf_op jit(solution)/shard_map/all_gather | solution.py:96
  134.1 2.2 multiply_reduce_fusion.4
  136.4 2.7 gather_fusion
  139.1 2.1 broadcast_multiply_fusion
  141.3 3.7 all-to-all-start
  145.0 1.0 copy.74
  145.9 9.9 %all-to-all-done = bf16[8,48,1024]{2,1,0:T(8,128)(2,1)S(1)} async-done(((bf16[8,48,1024]{2,1,0:T(8,128)(2,1)}), bf16[8,48,1024]{2,1,0:T(8,128)(2,1)S(1)}, u32[]{:S(2)}, u32[]{:S(2)}) %all-to-all-start) | async-done | bytes 786464 | tf_op jit(solution)/shard_map/all_to_all | solution.py:135
  155.8 0.9 copy-done.12
  156.7 1.4 copy.70
  158.1 5.8 fusion.55
  163.9 2.4 fusion.28
  166.3 2.7 convolution_convert_fusion.4
  169.0 1.5 copy.75
  170.5 3.5 all-to-all-start.3
  174.1 3.1 convolution_convert_fusion.5
  177.2 1.5 copy.71
  178.7 5.4 all-to-all-done.3
  184.1 0.9 copy-done.11
  185.0 3.5 all-to-all-start.1
  188.8 1.3 pad_clamp_fusion
  190.1 1.4 copy.76
  191.4 2.1 gather_fusion.2
  193.5 2.7 reshape.263
  196.2 2.5 reduce_sum.123
  198.7 0.7 multiply_reduce_fusion.2
  200.3 1.4 gather_fusion.1
  201.8 1.6 reshape.262
  203.4 2.7 multiply_reduce_fusion.1
  206.2 0.9 convert_add_fusion
  207.1 0.8 convolution_convert_fusion.6
  211.1 3.4 convolution_convert_fusion.1
  214.6 0.9 copy-done.23
  215.4 2.0 convolution_convert_fusion.3
  217.8 3.3 convolution_convert_fusion.2
  221.2 5.8 convolution_convert_fusion
  226.9 43.5 %reduce-scatter.3.cloned.1.call-done = bf16[512,2048]{1,0:T(8,128)(2,1)} async-done(((bf16[1024,2048]{1,0:T(8,128)(2,1)}), bf16[512,2048]{1,0:T(8,128)(2,1)}) %reduce-scatter.3.cloned.1.call-update) | async-done | bytes 2097168 | tf_op jit(solution)/shard_map/reduce_scatter | solution.py:229
  270.4 2.4 slice.80
  272.8 1.1 fusion.53
  273.9 31.1 %reduce-scatter.5.cloned.1.call-done = bf16[512,1024]{1,0:T(8,128)(2,1)} async-done(((bf16[1024,1024]{1,0:T(8,128)(2,1)}), bf16[512,1024]{1,0:T(8,128)(2,1)}) %reduce-scatter.5.cloned.1.call-update) | async-done | bytes 1048592 | tf_op jit(solution)/shard_map/reduce_scatter | solution.py:236
  307.0 0.8 fusion.56
  309.3 4.9 all-reduce.6
  314.4 33.6 %all-reduce.4 = (bf16[512]{0:T(512)(128)(2,1)S(1)}, bf16[512]{0:T(512)(128)(2,1)S(1)}) all-reduce(bf16[512]{0:T(512)(128)(2,1)S(1)} %dynamic-slice.1, bf16[512]{0:T(512)(128)(2,1)S(1)} %dynamic-slice.3), channel_id=1, replica_groups=mesh['rep'=16,'shard'=2] {'rep'}, use_global_device_ids=true, to_apply=%region_17.18 | all-reduce | flops 1024 | bytes 4096 | tf_op jit(solution)/shard_map/psum | solution.py:261
  349.1 0.9 fusion.15
  350.0 242.4 %all-reduce.9.cloned.1.call-done = (bf16[512,1024]{1,0:T(8,128)(2,1)}, bf16[512,512]{1,0:T(8,128)(2,1)}, bf16[512,512]{1,0:T(8,128)(2,1)}, bf16[512,1024]{1,0:T(...) async-done(((bf16[512,1024]{1,0:T(8,128)(2,1)}, bf16[512,512]{1,0:T(8,128)(2,1)}, bf16[512,512]{1,0:T(8,128)(2,1)}, bf16[512,1024]{1,0:T(8,128)(2,1)}, ...) | async-done | bytes 15728656 | tf_op jit(solution)/shard_map/psum | solution.py:262
  592.5 2.9 convert_element_type.198
  595.4 1.1 convert_element_type.199
  596.5 1.1 convert_element_type.200
  597.6 1.6 convert_element_type.202
  599.1 11.9 %convert_element_type.206 = f32[4,1024,1024]{2,1,0:T(8,128)} convert(bf16[4,1024,1024]{2,1,0:T(8,128)(2,1)} %get-tuple-element.20) | non-fusion elementwise | flops 4194304 | bytes 25165824 | tf_op jit(solution)/shard_map/convert_element_type | solution.py:267
  611.0 4.4 convert_element_type.208
  (209 shorter events, 15.5 us)
Async XLA Ops:
  7.2 2.2 copy-start.53
  7.2 3.8 copy-start.30
  7.2 42.2 %all-gather.7.cloned.1.call-start = ((), (), s32[]{:S(2)}) async-start(), calls=%async_computation.6 | async-start | bytes 1572864 | tf_op jit(solution)/shard_map/all_gather | solution.py:95
  7.9 57.0 %all-gather.9.cloned.1.call-start = ((), (), s32[]{:S(2)}) async-start(), calls=%async_computation.7 | async-start | bytes 1572864 | tf_op jit(solution)/shard_map/all_gather | solution.py:94
  8.7 90.9 %all-gather.11.cloned.1.call-start = ((), (), s32[]{:S(2)}) async-start(), calls=%async_computation.8 | async-start | bytes 3145728 | tf_op jit(solution)/shard_map/all_gather | solution.py:93
  10.9 1.2 copy-start.55
  12.9 34.2 %copy-start.54 = (s32[256,1]{0,1:T(1,128)}, s32[256,1]{0,1:T(1,128)S(1)}, u32[]{:S(2)}) copy-start(s32[256,1]{0,1:T(1,128)S(1)} %compare_select_fusion) | copy-start | bytes 3076
  12.9 7.5 %copy-start.56 = (bf16[512]{0:T(512)(128)(2,1)S(1)}, bf16[512]{0:T(512)(128)(2,1)}, u32[]{:S(2)}) copy-start(bf16[512]{0:T(512)(128)(2,1)} %param.18) | copy-start | bytes 3076
  12.9 27.7 %copy-start = (bf16[128,1024]{1,0:T(8,128)(2,1)S(1)}, bf16[128,1024]{1,0:T(8,128)(2,1)}, u32[]{:S(2)}) copy-start(bf16[128,1024]{1,0:T(8,128)(2,1)} %param.13) | copy-start | bytes 786436
  12.9 28.4 %copy-start.63 = (s32[128]{0:T(128)S(1)}, s32[128]{0:T(128)}, u32[]{:S(2)}) copy-start(s32[128]{0:T(128)} %param.14) | copy-start | bytes 1540
  12.9 28.4 %copy-start.57 = (bf16[512]{0:T(512)(128)(2,1)S(1)}, bf16[512]{0:T(512)(128)(2,1)}, u32[]{:S(2)}) copy-start(bf16[512]{0:T(512)(128)(2,1)} %param.23) | copy-start | bytes 3076
  15.5 125.7 %all-to-all-start.2 = ((bf16[8,48,1024]{2,1,0:T(8,128)(2,1)}), bf16[8,48,1024]{2,1,0:T(8,128)(2,1)S(1)}, u32[]{:S(2)}, u32[]{:S(2)}) async-start(bf16[8,48,1024]{2,1,0:T(8,128)(2,1)} %bitcast.25), calls=%async_computation.2 | async-start | bytes 1572864 | tf_op jit(solution)/shard_map/all_to_all | solution.py:153
  19.8 114.3 %all-gather.13.cloned.1.call-start = ((), (), s32[]{:S(2)}) async-start(), calls=%async_computation.9 | async-start | bytes 3145728 | tf_op jit(solution)/shard_map/all_gather | solution.py:96
  41.3 60.9 %copy-start.47 = (f32[128]{0:T(128)}, f32[128]{0:T(128)S(1)}, u32[]{:S(2)}) copy-start(f32[128]{0:T(128)S(1)} %fusion.37) | copy-start | bytes 1540
  49.4 52.8 %copy-start.40 = (f32[128,32]{0,1:T(8,128)}, f32[128,32]{0,1:T(8,128)S(1)}, u32[]{:S(2)}) copy-start(f32[128,32]{0,1:T(8,128)S(1)} %get-tuple-element.41) | copy-start | bytes 49156
  66.8 35.9 %copy-start.42 = (bf16[128,8,32]{0,2,1:T(8,128)(2,1)}, bf16[128,8,32]{0,2,1:T(8,128)(2,1)S(1)}, u32[]{:S(2)}) copy-start(bf16[128,8,32]{0,2,1:T(8,128)(2,1)S(1)} %get-tuple-element.37) | copy-start | bytes 196612
  66.8 35.9 %copy-start.44 = (bf16[128,8,32]{0,2,1:T(8,128)(2,1)}, bf16[128,8,32]{0,2,1:T(8,128)(2,1)S(1)}, u32[]{:S(2)}) copy-start(bf16[128,8,32]{0,2,1:T(8,128)(2,1)S(1)} %get-tuple-element.38) | copy-start | bytes 196612
  103.3 33.0 %copy-start.22 = (bf16[8,64,2,128]{3,1,2,0:T(8,128)(2,1)}, bf16[8,64,2,128]{3,1,2,0:T(8,128)(2,1)S(1)}, u32[]{:S(2)}) copy-start(bf16[8,64,2,128]{3,1,2,0:T(8,128)(2,1)S(1)} %convolution_convert_fusion.7) | copy-start | bytes 786436
  136.3 2.9 copy-start.61
  136.3 2.8 copy-start.50
  141.3 14.6 %all-to-all-start = ((bf16[8,48,1024]{2,1,0:T(8,128)(2,1)}), bf16[8,48,1024]{2,1,0:T(8,128)(2,1)S(1)}, u32[]{:S(2)}, u32[]{:S(2)}) async-start(bf16[8,48,1024]{2,1,0:T(8,128)(2,1)} %broadcast_multiply_fusion), calls=%async_computation | async-start | bytes 1572864 | tf_op jit(solution)/shard_map/all_to_all | solution.py:135
  156.7 7.2 %copy-start.1 = (bf16[4,512,1024]{2,1,0:T(8,128)(2,1)S(1)}, bf16[4,512,1024]{2,1,0:T(8,128)(2,1)}, u32[]{:S(2)}) copy-start(bf16[4,512,1024]{2,1,0:T(8,128)(2,1)} %param.25) | copy-start | bytes 12582916
  156.7 7.2 %copy-start.13 = (bf16[4,2,48,1024]{3,2,1,0:T(8,128)(2,1)S(1)}, bf16[4,2,48,1024]{3,2,1,0:T(8,128)(2,1)}, u32[]{:S(2)}) copy-start(bf16[4,2,48,1024]{3,2,1,0:T(8,128)(2,1)} %copy.74) | copy-start | bytes 2359300
  156.7 9.6 %slice-start = ((s8[8388608]{0:T(1024)(128)(4,1)}), s8[4194304]{0:T(1024)(128)(4,1)S(1)}, s32[]{:S(2)}) async-start(s8[8388608]{0:T(1024)(128)(4,1)} %bitcast.112), calls=%async_computation.13 | async-start | bytes 8388608
  158.1 5.8 copy-start.4
  158.1 8.2 %slice-start.1 = ((s8[8388608]{0:T(1024)(128)(4,1)}), s8[4194304]{0:T(1024)(128)(4,1)S(1)}, s32[]{:S(2)}) async-start(s8[8388608]{0:T(1024)(128)(4,1)} %bitcast.112), calls=%async_computation.14 | async-start | bytes 8388608
  166.3 2.7 copy-start.15
  166.3 2.7 copy-start.17
  170.5 13.6 %all-to-all-start.3 = ((bf16[4,96,1024]{2,0,1:T(4,128)(2,1)}), bf16[4,96,1024]{2,0,1:T(4,128)(2,1)S(1)}, u32[]{:S(2)}, u32[]{:S(2)}) async-start(bf16[4,96,1024]{2,0,1:T(4,128)(2,1)} %copy.75), calls=%async_computation.3 | async-start | bytes 1572864 | tf_op jit(solution)/shard_map/all_to_all | solution.py:165
  185.0 15.0 %all-to-all-start.1 = ((bf16[4,96,1024]{2,0,1:T(4,128)(2,1)}), bf16[4,96,1024]{2,0,1:T(4,128)(2,1)S(1)}, u32[]{:S(2)}, u32[]{:S(2)}) async-start(bf16[4,96,1024]{2,0,1:T(4,128)(2,1)} %copy.71), calls=%async_computation.1 | async-start | bytes 1572864 | tf_op jit(solution)/shard_map/all_to_all | solution.py:142
  188.5 81.9 %reduce-scatter.3.cloned.1.call-start = ((), (), s32[]{:S(2)}) async-start(), calls=%async_computation.10 | async-start | bytes 6291456 | tf_op jit(solution)/shard_map/reduce_scatter | solution.py:229
  193.5 5.2 copy-start.51
  193.5 5.9 copy-start.62
  198.7 1.3 copy-start.6
  200.3 3.1 copy-start.33
  201.7 4.4 copy-start.7
  201.7 4.4 copy-start.31
  201.7 4.4 copy-start.52
  201.7 4.4 copy-start.60
  203.4 3.7 copy-start.3
  209.0 1.1 copy-start.41
  209.0 1.1 copy-start.46
  209.5 1.6 copy-start.48
  210.1 4.3 copy-start.27
  214.5 3.3 copy-start.14
  214.5 3.3 copy-start.19
  214.5 90.5 %reduce-scatter.5.cloned.1.call-start = ((), (), s32[]{:S(2)}) async-start(), calls=%async_computation.11 | async-start | bytes 3145728 | tf_op jit(solution)/shard_map/reduce_scatter | solution.py:236
  217.5 3.7 copy-start.5
  217.5 3.7 copy-start.16
  217.5 375.0 %all-reduce.9.cloned.1.call-start = ((), (), s32[]{:S(2)}) async-start(), calls=%async_computation.12 | async-start | bytes 31457280 | tf_op jit(solution)/shard_map/psum | solution.py:262
  217.8 3.4 copy-start.18
  270.4 2.4 copy-start.24
  305.0 1.9 copy-start.2
  305.0 1.9 copy-start.21
  305.1 2.7 copy-start.26
  306.9 1.2 copy-start.10
  307.0 1.7 copy-start.9
  307.0 1.7 copy-start.28
  308.2 1.1 copy-start.49
  308.2 40.9 %copy-start.59 = (f32[128]{0:T(128)S(1)}, f32[128]{0:T(128)}, u32[]{:S(2)}) copy-start(f32[128]{0:T(128)} %copy-done.58) | copy-start | bytes 1540
  592.5 2.9 copy-start.35
  592.5 4.0 copy-start.34
  595.3 2.2 copy-start.29
  599.1 11.9 %copy-start.8 = (bf16[4,512,1024]{2,1,0:T(8,128)(2,1)S(1)}, bf16[4,512,1024]{2,1,0:T(8,128)(2,1)}, u32[]{:S(2)}) copy-start(bf16[4,512,1024]{2,1,0:T(8,128)(2,1)} %get-tuple-element.21) | copy-start | bytes 12582916
  (14 other events, 11.0 us)
Sparse Core Ops, SparseCore 0:
  9.5 32.4 all-gather.6
  43.6 21.2 all-gather.8
  66.5 33.0 all-gather.10
  101.0 33.0 all-gather.12
  214.6 55.7 reduce-scatter.2
  273.1 31.8 reduce-scatter.4
  311.5 280.9 all-reduce.8
where the time goes:
time: 631 us; the launch traced here: 623 us
  waiting for transfers between devices  412 us (65%)
  blocking collectives  63 us (10%)
  matrix products  41.3 us (7%)
  other arithmetic  41 us (6%)
  local copies, waits for them, and re-layouts  33.1 us (5%)
  between operations  16.2 us (3%)
  starting transfers between devices  15.7 us (2%)
    psum x1, waiting for transfers between devices, per_device(): lax.psum(owned_query.astype(jnp.bfloat16), 'rep').astype(jnp.float32)  242 us
    reduce_scatter x1, waiting for transfers between devices, per_device(): lax.psum_scatter(jnp.dot(normed_low.T, projected, preferred_element_type=...  43.5 us
    psum x1, blocking collectives, per_device(): lax.psum(owned_former.astype(jnp.bfloat16), 'rep').astype(jnp.float32)  33.6 us
    all_gather x1, waiting for transfers between devices, per_device(): lax.all_gather(w_query, 'shard', axis=0, tiled=True)  32.8 us
    reduce_scatter x1, waiting for transfers between devices, per_device(): lax.psum_scatter(proj_grad.astype(jnp.bfloat16), 'shard', scatter_dimensi...  31.1 us
    all_gather x1, waiting for transfers between devices, per_device(): lax.all_gather(w_out, 'shard', axis=0, tiled=True)  30.8 us
    all_gather x1, blocking collectives, per_device(): lax.all_gather(attn_gain, 'shard', axis=0, tiled=True)  20.1 us
    all_gather x1, waiting for transfers between devices, per_device(): lax.all_gather(key_weight, 'shard', axis=0, tiled=True)  13.8 us
  transfers between devices with their start and end apart: 11, of which 8 were waited for; matrix products, arithmetic and copies ran while one was open for 10% of the time, Pallas kernels for 0%

commit v1 on v0

--- a/solution.py
+++ b/solution.py
@@ -281,34 +281,332 @@
     )
 
 
+PAIR = [(0, 1), (1, 0)]
+
+
+def swap(values, axis):
+    return lax.ppermute(values, axis, PAIR)
+
+
+def bf(values):
+    return values.astype(jnp.bfloat16)
+
+
+def f32(values):
+    return values.astype(jnp.float32)
+
+
+def dot(left, right):
+    return jnp.dot(left, right, preferred_element_type=jnp.float32)
+
+
+def dot_nt(left, right):
+    return lax.dot_general(left, right, (((1,), (1,)), ((), ())), preferred_element_type=jnp.float32)
+
+
+def dot_tn(left, right):
+    return lax.dot_general(left, right, (((0,), (0,)), ((), ())), preferred_element_type=jnp.float32)
+
+
+def ein(spec, left, right):
+    return jnp.einsum(spec, left, right, preferred_element_type=jnp.float32)
+
+
+def gather_group(rows):
+    half = rows.shape[1] // 2
+    first, second = rows[:, :half], rows[:, half:]
+    first = jnp.stack([first, swap(first, "x")])
+    second = jnp.stack([second, swap(second, "y")])
+    first = jnp.stack([first, swap(first, "y")])
+    second = jnp.stack([second, swap(second, "x")], axis=1)
+    halves = []
+    for part in (first, second):
+        both = jnp.stack([part, swap(part, "core")])
+        halves.append(both.reshape((8,) + rows.shape[:1] + (half,)))
+    return halves
+
+
+def scatter_group(parts):
+    half = parts.shape[-1] // 2
+    kept = bf(f32(parts[0]) + f32(swap(parts[1], "core")))
+    first, second = kept[..., :half], kept[..., half:]
+    first = bf(f32(first[:, 0]) + f32(swap(first[:, 1], "x")))
+    second = bf(f32(second[0]) + f32(swap(second[1], "y")))
+    first = f32(first[0]) + f32(swap(first[1], "y"))
+    second = f32(second[0]) + f32(swap(second[1], "x"))
+    return jnp.concatenate([first, second], axis=1)
+
+
+def per_device_split(
+    tokens,
+    positions,
+    routes,
+    gates,
+    cotangent,
+    attn_gain,
+    w_query,
+    key_weight,
+    value_weight,
+    w_out,
+    ffn_gain,
+    w_gate_up,
+    w_down,
+):
+    length, width = tokens.shape
+    half_width = width // 2
+    heads = KEY_VALUE_HEADS // 2
+    grouped = QUERY_HEADS // KEY_VALUE_HEADS
+    q_cols = heads * grouped * HEAD_DIM
+    k_cols = heads * HEAD_DIM
+    here = lax.axis_index("x")
+    member = lax.axis_index("y") * 2 + lax.axis_index("core")
+    expert = here * 4 + member
+
+    def mine(values, axis):
+        size = values.shape[axis] // 2
+        return lax.dynamic_slice_in_dim(values, here * size, size, axis)
+
+    def other(values, axis):
+        size = values.shape[axis] // 2
+        return lax.dynamic_slice_in_dim(values, (1 - here) * size, size, axis)
+
+    def ordered(own, received, axis):
+        return jnp.where(
+            here == 0,
+            jnp.concatenate([own, received], axis),
+            jnp.concatenate([received, own], axis),
+        )
+
+    def turned(values):
+        return jnp.concatenate([values[length:], values[:length]], axis=0)
+
+    inputs = f32(tokens)
+    inverse = lax.rsqrt(jnp.mean(inputs * inputs, axis=-1, keepdims=True) + RMS_EPS)
+    own_cols = mine(tokens, 1)
+    their_cols = swap(other(tokens, 1), "x")
+    facts = jnp.concatenate(
+        [
+            gates.T,
+            f32(routes).T,
+            f32(positions)[None],
+            inverse.T,
+            f32(ffn_gain).reshape(-1, length),
+        ],
+        axis=0,
+    )
+    facts = jnp.pad(facts, ((0, -facts.shape[0] % 8), (0, 0)))
+    their_facts = swap(facts, "x")
+    facts_pair = jnp.stack([facts, their_facts])
+    facts_quad = jnp.stack([facts_pair, swap(facts_pair, "y")])
+    facts_all = jnp.stack([facts_quad, swap(facts_quad, "core")]).reshape((8,) + facts.shape)
+
+    gain_one = f32(attn_gain)
+    normed = jnp.concatenate(
+        [
+            bf(f32(own_cols) * inverse * gain_one),
+            bf(f32(their_cols) * their_facts[5][:, None] * gain_one),
+        ],
+        axis=0,
+    )
+    partial = [dot(normed, w) for w in (w_query, key_weight, value_weight)]
+    sent = jnp.concatenate([bf(other(p, 1)) for p in partial], axis=1)
+    arrived = turned(swap(sent, "x"))
+    kept = jnp.concatenate([mine(p, 1) for p in partial], axis=1) + f32(arrived)
+    place = jnp.stack([facts[4], their_facts[4]])
+    half_dim = HEAD_DIM // 2
+    frequency = ROPE_BASE ** (-(2.0 * jnp.arange(half_dim, dtype=jnp.float32)) / HEAD_DIM)
+    angles = place[:, :, None] * frequency
+    cosine, sinusoid = jnp.cos(angles)[:, :, None, :], jnp.sin(angles)[:, :, None, :]
+    q = bf(apply_rotary(kept[:, :q_cols].reshape(2, length, -1, HEAD_DIM), cosine, sinusoid))
+    k = bf(
+        apply_rotary(
+            kept[:, q_cols : q_cols + k_cols].reshape(2, length, -1, HEAD_DIM), cosine, sinusoid
+        )
+    )
+    v = bf(kept[:, q_cols + k_cols :]).reshape(2, length, heads, HEAD_DIM)
+    q = q.reshape(2, length, heads, grouped, HEAD_DIM)
+    causal = jnp.arange(length)[:, None] >= jnp.arange(length)[None, :]
+    scores = jnp.where(causal, ATT_MULT * ein("sqhgd,skhd->shgqk", q, k), -1e30)
+    probs = jax.nn.softmax(scores, axis=-1)
+    probs_low = bf(probs)
+    attended = bf(ein("shgqk,skhd->sqhgd", probs_low, v)).reshape(2 * length, q_cols)
+    branch = dot(attended, w_out)
+    hidden = inputs + RES_MULT * (branch[:length] + f32(swap(bf(branch[length:]), "x")))
+    gain_rows = half_width // length
+    gain_two = ordered(
+        facts[6 : 6 + gain_rows].reshape(-1), their_facts[6 : 6 + gain_rows].reshape(-1), 0
+    )
+    inverse_two = lax.rsqrt(jnp.mean(hidden * hidden, axis=-1, keepdims=True) + RMS_EPS)
+    second = bf(hidden * inverse_two * gain_two)
+
+    match = f32(facts_all[:, 2:4] == f32(expert))
+    taken = jnp.sum(match, axis=1)
+    gate = jnp.sum(facts_all[:, 0:2] * match, axis=1)
+    rank = dot(bf(taken), bf(jnp.arange(length)[:, None] < jnp.arange(length)[None, :]))
+    slots = jnp.arange(CAP, dtype=jnp.float32)
+    pick = bf((rank[:, None, :] == slots[None, :, None]) & (taken[:, None, :] > 0))
+    w_in = lax.dynamic_index_in_dim(w_gate_up, member, 0, keepdims=False)
+    w_back = lax.dynamic_index_in_dim(w_down, member, 0, keepdims=False)
+
+    def dispatch(values):
+        return bf(ein("sct,std->scd", pick, values)).reshape(8 * CAP, -1)
+
+    def undispatch(values):
+        return ein("sct,scd->std", pick, values.reshape(8, CAP, -1))
+
+    upstream = f32(cotangent)
+    later, _ = lax.optimization_barrier((cotangent, arrived))
+    out_grad = jnp.concatenate(
+        [dispatch(bf(gate[:, :, None] * (RES_MULT * f32(part)))) for part in gather_group(later)],
+        axis=1,
+    )
+    act_grad = dot_nt(out_grad, w_back)
+    rows = jnp.concatenate([dispatch(part) for part in gather_group(second)], axis=1)
+    gate_up = dot(rows, w_in)
+    front, back = gate_up[:, :F], gate_up[:, F:]
+    sigmoid = jax.nn.sigmoid(front)
+    silu = front * sigmoid
+    activated = bf(silu * back)
+    inner = jnp.concatenate(
+        [
+            bf(act_grad * back * (sigmoid * (1.0 + front * (1.0 - sigmoid)))),
+            bf(act_grad * silu),
+        ],
+        axis=1,
+    )
+    rows_grad = bf(dot_nt(inner, w_in))
+    shape = (2, 2, 2, length, width)
+    second_grad = scatter_group(bf(undispatch(rows_grad)).reshape(shape))
+    grad_down = bf(dot_tn(activated, out_grad))
+    grad_gate_up = bf(dot_tn(rows, inner))
+    expert_out = bf(dot(activated, w_back))
+    combined = scatter_group(bf(gate[:, :, None] * undispatch(expert_out)).reshape(shape))
+    output = bf(hidden + RES_MULT * combined)
+
+    cotan = second_grad * gain_two
+    hidden_grad = (
+        upstream
+        + inverse_two * cotan
+        - hidden * inverse_two**3 * jnp.mean(cotan * hidden, axis=-1, keepdims=True)
+    )
+    gain_grad = jnp.sum(second_grad * hidden * inverse_two, axis=0, keepdims=True)
+    branch_grad = bf(RES_MULT * hidden_grad)
+    both = jnp.concatenate([branch_grad, bf(jnp.pad(gain_grad, ((0, 15), (0, 0))))], axis=0)
+    theirs = swap(both, "x")
+    grad_ffn = mine(gain_grad + f32(theirs[length : length + 1]), 1)
+    branch_pair = jnp.concatenate([branch_grad, theirs[:length]], axis=0)
+    att_grad = bf(dot_nt(branch_pair, w_out)).reshape(2, length, heads, grouped, HEAD_DIM)
+    grad_out = bf(dot_tn(attended, branch_pair))
+    probs_grad = ein("sqhgd,skhd->shgqk", att_grad, v)
+    inner_sum = jnp.sum(probs * probs_grad, axis=-1, keepdims=True)
+    score_grad = bf(probs * (probs_grad - inner_sum))
+    v_grad = bf(ein("shgqk,sqhgd->skhd", probs_low, att_grad)).reshape(2 * length, -1)
+    q_grad = ATT_MULT * ein("shgqk,skhd->sqhgd", score_grad, k)
+    k_grad = ATT_MULT * ein("shgqk,sqhgd->skhd", score_grad, q)
+    q_grad = bf(apply_rotary(q_grad.reshape(2, length, -1, HEAD_DIM), cosine, -sinusoid))
+    k_grad = bf(apply_rotary(k_grad, cosine, -sinusoid))
+    turned_grad = jnp.concatenate(
+        [q_grad.reshape(2 * length, -1), k_grad.reshape(2 * length, -1), v_grad], axis=1
+    )
+    their_grad = turned(swap(turned_grad, "x"))
+    pieces = []
+    for lo, hi in ((0, q_cols), (q_cols, q_cols + k_cols), (q_cols + k_cols, q_cols + 2 * k_cols)):
+        pieces.append(ordered(turned_grad[:, lo:hi], their_grad[:, lo:hi], 1))
+    normed_grad = (
+        dot_nt(pieces[0], w_query) + dot_nt(pieces[1], key_weight) + dot_nt(pieces[2], value_weight)
+    )
+    weighted = normed_grad * gain_one
+    full = ordered(weighted[:length], f32(swap(bf(weighted[length:]), "x")), 1)
+    input_grad = bf(
+        hidden_grad
+        + inverse * full
+        - inputs * inverse**3 * jnp.mean(full * inputs, axis=-1, keepdims=True)
+    )
+    scaled = jnp.concatenate(
+        [f32(own_cols) * inverse, f32(their_cols) * their_facts[5][:, None]], axis=0
+    )
+    grad_attn = jnp.sum(normed_grad * scaled, axis=0, keepdims=True)
+    grads = [bf(dot_tn(normed, piece)) for piece in pieces]
+    return (output, input_grad, grad_attn, grad_ffn, grads, grad_out, grad_gate_up, grad_down)
+
+
+def split_step(*arrays):
+    output, input_grad, grad_attn, grad_ffn, grads, grad_out, grad_gate_up, grad_down = (
+        per_device_split(*arrays)
+    )
+    def over_group(values):
+        part = lax.psum_scatter(values, "z", scatter_dimension=0, tiled=True)
+        whole = lax.all_gather(part, ("y", "core", "z"), axis=0, tiled=True)
+        return f32(whole).reshape((4,) + values.shape)
+
+    rows = grads[0].shape[0]
+    sums = jnp.concatenate(
+        [
+            jnp.concatenate(list(grads) + [grad_out], axis=1),
+            jnp.pad(
+                bf(jnp.concatenate([grad_attn, grad_ffn], axis=0)),
+                ((0, 14), (0, sum(g.shape[1] for g in grads) + grad_out.shape[1] - rows)),
+            ),
+        ],
+        axis=0,
+    )
+    sum_down = over_group(grad_down)
+    sum_gate_up = over_group(grad_gate_up)
+    sums = f32(lax.psum(sums, ("z", "y", "core")))
+    cuts, at = [], 0
+    for g in list(grads) + [grad_out]:
+        cuts.append(sums[:rows, at : at + g.shape[1]])
+        at += g.shape[1]
+    return (
+        output,
+        input_grad,
+        sums[rows, :rows],
+        cuts[0],
+        cuts[1],
+        cuts[2],
+        cuts[3],
+        sums[rows + 1, :rows],
+        sum_gate_up,
+        sum_down,
+    )
+
+
 def solution(mesh):
+    replicas, shards = mesh.devices.shape
+    if shards == 2 and EXPERTS == 8 and replicas % 4 == 0:
+        split = jax.sharding.Mesh(
+            mesh.devices.reshape(replicas // 4, 2, 2, 2), ("z", "y", "core", "x")
+        )
+        return mapped(split_step, split, ("z", "y", "core", "x"), "x")
+    return mapped(per_device, mesh, ("rep", "shard"), "shard")
+
+
+def mapped(step, mesh, every, shard):
     in_specs = (
-        P(("rep", "shard"), None),
-        P(("rep", "shard")),
-        P(("rep", "shard"), None),
-        P(("rep", "shard"), None),
-        P(("rep", "shard"), None),
-        P("shard"),
-        P("shard", None),
-        P("shard", None),
-        P("shard", None),
-        P("shard", None),
-        P("shard"),
-        P("shard", None, None),
-        P("shard", None, None),
+        P(every, None),
+        P(every),
+        P(every, None),
+        P(every, None),
+        P(every, None),
+        P(shard),
+        P(shard, None),
+        P(shard, None),
+        P(shard, None),
+        P(shard, None),
+        P(shard),
+        P(shard, None, None),
+        P(shard, None, None),
     )
     out_specs = (
-        P(("rep", "shard"), None),
-        P(("rep", "shard"), None),
-        P("shard"),
-        P("shard", None),
-        P("shard", None),
-        P("shard", None),
-        P("shard", None),
-        P("shard"),
-        P("shard", None, None),
-        P("shard", None, None),
-    )
-    return jax.shard_map(
-        per_device, mesh=mesh, in_specs=in_specs, out_specs=out_specs, check_vma=False
-    )
+        P(every, None),
+        P(every, None),
+        P(shard),
+        P(shard, None),
+        P(shard, None),
+        P(shard, None),
+        P(shard, None),
+        P(shard),
+        P(shard, None, None),
+        P(shard, None, None),
+    )
+    return jax.shard_map(step, mesh=mesh, in_specs=in_specs, out_specs=out_specs, check_vma=False)

time: 631 us -> 408 us (0.65); the launches traced: 623 us -> 407 us
  waiting for transfers between devices: 412 us -> 265 us
  blocking collectives: 63 us -> 0 us
  matrix products: 41.3 us -> 26.9 us
  starting transfers between devices: 15.7 us -> 28.9 us
  local copies, waits for them, and re-layouts: 33.1 us -> 25.7 us
    psum x1, waiting for transfers between devices: 242 us -> 88.2 us  [split_step(): sums = f32(lax.psum(sums, ('z', 'y', 'core')))]
    reduce_scatter x2, waiting for transfers between devices: 74.6 us -> 13.9 us  [over_group(): part = lax.psum_scatter(values, 'z', scatter_dimension=0, tiled=True)]
    ppermute x0 -> x31, waiting for transfers between devices: none -> 49.9 us  [swap(): return lax.ppermute(values, axis, PAIR)]
    all_gather x4 -> x2, waiting for transfers between devices: 77.4 us -> 113 us  [over_group(): whole = lax.all_gather(part, ('y', 'core', 'z'), axis=0, tiled=True)]
    psum x1 -> x0, blocking collectives: 33.6 us -> none  [per_device(): lax.psum(owned_former.astype(jnp.bfloat16), 'rep').astype(jnp.float32)]
    ppermute x0 -> x31, starting transfers between devices: none -> 28.7 us  [swap(): return lax.ppermute(values, axis, PAIR)]
    all_gather x2 -> x0, blocking collectives: 24.5 us -> none  [the longest x1 20.1 us: per_device(): lax.all_gather(attn_gain, 'shard', axis=0, tiled=True)]
    reshape x0 -> x2, other arithmetic: none -> 18.3 us  [over_group(): return f32(whole).reshape((4,) + values.shape)]
  transfers between devices with their start and end apart: 11 -> 36, of which waited for: 8 -> 22; matrix products, arithmetic and copies ran while one was open for 10% -> 18% of each run, Pallas kernels for 0% -> 0%
where the time goes in v1:
time: 408 us; the launch traced here: 407 us
  waiting for transfers between devices  265 us (65%)
  other arithmetic  43.4 us (11%)
  starting transfers between devices  28.9 us (7%)
  matrix products  26.9 us (7%)
  local copies, waits for them, and re-layouts  25.7 us (6%)
  between operations  17 us (4%)
    all_gather x2, waiting for transfers between devices, over_group(): whole = lax.all_gather(part, ('y', 'core', 'z'), axis=0, tiled=True)  113 us
    psum x1, waiting for transfers between devices, split_step(): sums = f32(lax.psum(sums, ('z', 'y', 'core')))  88.2 us
    ppermute x31, waiting for transfers between devices, swap(): return lax.ppermute(values, axis, PAIR)  49.9 us
    ppermute x31, starting transfers between devices, swap(): return lax.ppermute(values, axis, PAIR)  28.7 us
    reshape x2, other arithmetic, over_group(): return f32(whole).reshape((4,) + values.shape)  18.3 us
    reduce_scatter x2, waiting for transfers between devices, over_group(): part = lax.psum_scatter(values, 'z', scatter_dimension=0, tiled=True)  13.9 us
    dot_general x11, matrix products, ein(): return jnp.einsum(spec, left, right, preferred_element_type=jnp.float32)  10.5 us
  transfers between devices with their start and end apart: 36, of which 22 were waited for; matrix products, arithmetic and copies ran while one was open for 18% of the time, Pallas kernels for 0%

profile of v1, /device:TPU:0, one launch (start us, length us, event | category | flops | bytes accessed | tf_op | source)
XLA Modules:
  0.0 407.2 jit_solution(17880420846887015424)
XLA Ops:
  8.1 1.0 constant_dynamic-slice_fusion.5
  9.2 3.0 collective-permute-start
  12.2 1.1 fusion.37
  16.7 1.7 slice_bitcast_fusion.21
  18.4 2.0 collective-permute-start.20
  20.4 1.5 collective-permute-start.17
  23.2 1.7 convert_multiply_fusion.6
  25.8 3.0 collective-permute-done.4
  33.5 1.6 fusion.125
  35.2 1.5 collective-permute-start.21
  36.7 1.6 fusion.126
  38.9 8.2 %collective-permute-done.2 = bf16[256,1024]{1,0:T(8,128)(2,1)S(1)} collective-permute-done((bf16[256,1024]{1,0:T(8,128)(2,1)S(1)}, bf16[256,1024]{1,0:T(8,128)(2,1)S(1)}, u32[]{:S(2)}, u32[]{:S(2)}) %collective-permute-start.2) | collective-permute-done | bytes 524320 | tf_op jit(solution)/shard_map/ppermute | solution.py:288
  51.4 2.5 fusion.147
  54.5 2.5 fusion.19
  57.0 1.2 copy.55
  59.3 1.0 fusion.129
  60.4 1.0 fusion.130
  62.0 3.6 collective-permute-done.3
  67.2 3.9 collective-permute-done.9
  72.8 1.8 collective-permute-start.7
  74.5 2.9 collective-permute-done.10
  77.8 1.5 collective-permute-done.7
  80.3 1.0 collective-permute-done.8
  82.1 1.0 fusion.7
  83.1 1.2 copy-done.35
  85.2 1.0 fusion.12
  87.0 1.5 fusion.139
  90.4 1.1 fusion.140
  91.5 1.7 convolution_convert_fusion.2
  93.3 1.9 fusion.1
  96.2 1.5 collective-permute-start.26
  97.7 1.6 fusion.4
  99.3 1.6 collective-permute-start.13
  101.3 3.2 collective-permute-done.24
  105.6 1.3 collective-permute-start.27
  106.9 1.8 collective-permute-start.25
  108.6 1.5 collective-permute-done.13
  110.1 0.9 collective-permute-done.15
  111.2 1.3 collective-permute-start.16
  112.5 1.8 collective-permute-start.14
  114.6 1.7 collective-permute-done.16
  116.3 1.2 collective-permute-done.14
  117.6 1.2 multiply_convert_fusion.5
  119.8 2.6 convolution_convert_fusion
  122.5 3.2 collective-permute-done.28
  125.7 1.0 slice.308
  126.7 1.7 convolution_convert_fusion.12
  129.1 1.8 multiply_reduce_fusion
  132.9 1.8 fusion.23
  134.9 1.3 fusion.21
  138.4 8.5 %collective-permute-done.29 = bf16[256,1024]{0,1:T(8,128)(2,1)S(1)} collective-permute-done((bf16[256,1024]{0,1:T(8,128)(2,1)S(1)}, bf16[256,1024]{0,1:T(8,128)(2,1)S(1)}, u32[]{:S(2)}, u32[]{:S(2)}) %collective-permute-start.29) | collective-permute-done | bytes 524320 | tf_op jit(solution)/shard_map/ppermute | solution.py:288
  149.8 2.9 pad_maximum_fusion
  153.5 13.9 %reduce-scatter.3.cloned.1.call-done = bf16[256,1024]{1,0:T(8,128)(2,1)} async-done(((bf16[1024,1024]{1,0:T(8,128)(2,1)}), bf16[256,1024]{1,0:T(8,128)(2,1)}) %reduce-scatter.3.cloned.1.call-update) | async-done | bytes 524304 | tf_op jit(solution)/shard_map/reduce_scatter | solution.py:538
  167.4 1.5 collective-permute-start.30
  168.9 3.5 collective-permute-done.30
  172.6 0.9 fusion.40
  173.6 88.2 %all-reduce.5.cloned.1.call-done = bf16[528,3072]{1,0:T(8,128)(2,1)} async-done(((bf16[528,3072]{1,0:T(8,128)(2,1)}), bf16[528,3072]{1,0:T(8,128)(2,1)}) %all-reduce.5.cloned.1.call-update) | async-done | bytes 3244048 | tf_op jit(solution)/shard_map/psum | solution.py:555
  261.8 1.4 fusion.136
  263.2 3.0 fusion.138
  266.1 2.5 fusion.137
  268.6 44.5 %all-gather.5.cloned.1.call-done = bf16[2048,1024]{1,0:T(8,128)(2,1)} async-done(((bf16[128,1024]{1,0:T(8,128)(2,1)}), bf16[2048,1024]{1,0:T(8,128)(2,1)}) %all-gather.5.cloned.1.call-update) | async-done | bytes 4194320 | tf_op jit(solution)/shard_map/all_gather | solution.py:539
  313.1 6.6 %convert.87 = f32[4,512,1024]{2,1,0:T(8,128)} convert(bf16[4,512,1024]{2,1,0:T(8,128)(2,1)} %bitcast.279) | non-fusion elementwise | flops 2097152 | bytes 12582912 | tf_op jit(solution)/shard_map/reshape | solution.py:540
  319.8 68.1 %all-gather.3.cloned.1.call-done = bf16[4096,1024]{1,0:T(8,128)(2,1)} async-done(((bf16[256,1024]{1,0:T(8,128)(2,1)}), bf16[4096,1024]{1,0:T(8,128)(2,1)}) %all-gather.3.cloned.1.call-update) | async-done | bytes 8388624 | tf_op jit(solution)/shard_map/all_gather | solution.py:539
  387.9 11.7 %convert.86 = f32[4,1024,1024]{2,1,0:T(8,128)} convert(bf16[4,1024,1024]{2,1,0:T(8,128)(2,1)} %bitcast.278) | non-fusion elementwise | flops 4194304 | bytes 25165824 | tf_op jit(solution)/shard_map/reshape | solution.py:540
  (255 shorter events, 38.8 us)
Async XLA Ops:
  8.0 23.6 %copy-start = (bf16[512,1024]{1,0:T(8,128)(2,1)S(1)}, bf16[512,1024]{1,0:T(8,128)(2,1)}, u32[]{:S(2)}) copy-start(bf16[512,1024]{1,0:T(8,128)(2,1)} %param.19) | copy-start | bytes 3145732
  8.0 23.0 %copy-start.7 = (bf16[512,512]{1,0:T(8,128)(2,1)S(1)}, bf16[512,512]{1,0:T(8,128)(2,1)}, u32[]{:S(2)}) copy-start(bf16[512,512]{1,0:T(8,128)(2,1)} %param.21) | copy-start | bytes 1572868
  8.0 144.9 %reduce-scatter.5.cloned.1.call-start = ((), (), s32[]{:S(2)}) async-start(), calls=%async_computation.5 | async-start | bytes 1310720 | tf_op jit(solution)/shard_map/reduce_scatter | solution.py:538
  9.1 22.2 %copy-start.9 = (bf16[512,512]{1,0:T(8,128)(2,1)S(1)}, bf16[512,512]{1,0:T(8,128)(2,1)}, u32[]{:S(2)}) copy-start(bf16[512,512]{1,0:T(8,128)(2,1)} %param.20) | copy-start | bytes 1572868
  9.2 21.0 %collective-permute-start = (bf16[128,512]{1,0:T(8,128)(2,1)S(1)}, bf16[128,512]{1,0:T(8,128)(2,1)S(1)}, u32[]{:S(2)}, u32[]{:S(2)}) collective-permute-start(bf16[128,512]{1,0:T(8,128)(2,1)S(1)} %constant_dynamic-slice_fusion.5), channel_id=1, source_target_pairs={{0,1},{1,0},{2,3},{3,2},{4,5},{5,4},{6,7},{7,6},{8,9},{9,8},{10,11... | collective-permute-start | bytes 393224 | tf_op jit(solution)/shard_map/ppermute | solution.py:288
  15.1 9.8 %copy-start.32 = (f32[128]{0:T(128)}, f32[128]{0:T(128)S(1)}, u32[]{:S(2)}) copy-start(f32[128]{0:T(128)S(1)} %get-tuple-element.17) | copy-start | bytes 1540
  16.6 8.3 %collective-permute-start.1 = (f32[16,128]{1,0:T(8,128)S(1)}, f32[16,128]{1,0:T(8,128)S(1)}, u32[]{:S(2)}, u32[]{:S(2)}) collective-permute-start(f32[16,128]{1,0:T(8,128)S(1)} %get-tuple-element.93), channel_id=1, source_target_pairs={{0,1},{1,0},{2,3},{3,2},{4,5},{5,4},{6,7},{7,6},{8,9},{9,8},{10,11... | collective-permute-start | bytes 24584 | tf_op jit(solution)/shard_map/ppermute | solution.py:288
  18.4 14.4 %collective-permute-start.20 = (bf16[128,512]{1,0:T(8,128)(2,1)S(1)}, bf16[128,512]{1,0:T(8,128)(2,1)S(1)}, u32[]{:S(2)}, u32[]{:S(2)}) collective-permute-start(bf16[128,512]{1,0:T(8,128)(2,1)S(1)} %get-tuple-element.74), channel_id=1, source_target_pairs={{0,4},{4,0},{1,5},{5,1},{2,6},{6,2},{3,7},{7,3},{8,12},{12,8},{9,1... | collective-permute-start | bytes 393224 | tf_op jit(solution)/shard_map/ppermute | solution.py:288
  20.4 16.2 %collective-permute-start.17 = (bf16[128,512]{1,0:T(8,128)(2,1)}, bf16[128,512]{1,0:T(8,128)(2,1)}, u32[]{:S(2)}, u32[]{:S(2)}) collective-permute-start(bf16[128,512]{1,0:T(8,128)(2,1)} %get-tuple-element.75), channel_id=1, source_target_pairs={{0,1},{1,0},{2,3},{3,2},{4,5},{5,4},{6,7},{7,6},{8,9},{9,8},{10,11... | collective-permute-start | bytes 393224 | tf_op jit(solution)/shard_map/ppermute | solution.py:288
  23.2 8.4 %copy-start.26 = (f32[512]{0:T(512)}, f32[512]{0:T(512)S(1)}, u32[]{:S(2)}) copy-start(f32[512]{0:T(512)S(1)} %convert_element_type.305) | copy-start | bytes 6148
  25.0 3.8 collective-permute-start.4
  28.8 1.2 collective-permute-start.5
  31.6 5.0 %copy-start.11 = (bf16[1,128,512]{2,1,0:T(8,128)(2,1)S(1)}, bf16[1,128,512]{2,1,0:T(8,128)(2,1)}, u32[]{:S(2)}) copy-start(bf16[1,128,512]{2,1,0:T(8,128)(2,1)} %get-tuple-element.72) | copy-start | bytes 393220
  32.3 14.9 %collective-permute-start.2 = (bf16[256,1024]{1,0:T(8,128)(2,1)S(1)}, bf16[256,1024]{1,0:T(8,128)(2,1)S(1)}, u32[]{:S(2)}, u32[]{:S(2)}) collective-permute-start(bf16[256,1024]{1,0:T(8,128)(2,1)S(1)} %pad_maximum_fusion.10), channel_id=1, source_target_pairs={{0,1},{1,0},{2,3},{3,2},{4,5},{5,4},{6,7},{7,6},{8,9},{9,8},{10,11... | collective-permute-start | bytes 1572872 | tf_op jit(solution)/shard_map/ppermute | solution.py:288
  35.2 24.1 %collective-permute-start.21 = (bf16[2,128,512]{2,1,0:T(8,128)(2,1)}, bf16[2,128,512]{2,1,0:T(8,128)(2,1)}, u32[]{:S(2)}, u32[]{:S(2)}) collective-permute-start(bf16[2,128,512]{2,1,0:T(8,128)(2,1)} %get-tuple-element.77), channel_id=1, source_target_pairs={{0,1},{1,0},{2,3},{3,2},{4,5},{5,4},{6,7},{7,6},{8,9},{9,8},{10,11... | collective-permute-start | bytes 786440 | tf_op jit(solution)/shard_map/ppermute | solution.py:288
  38.3 22.1 %collective-permute-start.18 = (bf16[2,128,512]{2,1,0:T(8,128)(2,1)}, bf16[2,128,512]{2,1,0:T(8,128)(2,1)}, u32[]{:S(2)}, u32[]{:S(2)}) collective-permute-start(bf16[2,128,512]{2,1,0:T(8,128)(2,1)} %get-tuple-element.71), channel_id=1, source_target_pairs={{0,4},{4,0},{1,5},{5,1},{2,6},{6,2},{3,7},{7,3},{8,12},{12,8},{9,1... | collective-permute-start | bytes 786440 | tf_op jit(solution)/shard_map/ppermute | solution.py:288
  51.4 5.6 %copy-start.17 = (bf16[2,128,4,32]{1,3,2,0:T(8,128)(2,1)}, bf16[2,128,4,32]{1,3,2,0:T(8,128)(2,1)S(1)}, u32[]{:S(2)}) copy-start(bf16[2,128,4,32]{1,3,2,0:T(8,128)(2,1)S(1)} %get-tuple-element.66) | copy-start | bytes 196612
  51.4 5.6 %copy-start.19 = (bf16[2,128,4,32]{1,3,2,0:T(8,128)(2,1)}, bf16[2,128,4,32]{1,3,2,0:T(8,128)(2,1)S(1)}, u32[]{:S(2)}) copy-start(bf16[2,128,4,32]{1,3,2,0:T(8,128)(2,1)S(1)} %get-tuple-element.67) | copy-start | bytes 196612
  54.5 3.7 copy-start.5
  56.9 2.4 copy-start.29
  58.7 6.9 %copy-start.2 = (bf16[128,1024]{1,0:T(8,128)(2,1)S(1)}, bf16[128,1024]{1,0:T(8,128)(2,1)}, u32[]{:S(2)}) copy-start(bf16[128,1024]{1,0:T(8,128)(2,1)} %param.13) | copy-start | bytes 786436
  58.7 6.9 %collective-permute-start.3 = (bf16[128,1024]{1,0:T(8,128)(2,1)S(1)}, bf16[128,1024]{1,0:T(8,128)(2,1)S(1)}, u32[]{:S(2)}, u32[]{:S(2)}) collective-permute-start(bf16[128,1024]{1,0:T(8,128)(2,1)S(1)} %slice.410), channel_id=1, source_target_pairs={{0,1},{1,0},{2,3},{3,2},{4,5},{5,4},{6,7},{7,6},{8,9},{9,8},{10,11... | collective-permute-start | bytes 786440 | tf_op jit(solution)/shard_map/ppermute | solution.py:288
  60.4 6.7 %collective-permute-start.22 = (bf16[2,2,128,512]{3,2,1,0:T(8,128)(2,1)S(1)}, bf16[2,2,128,512]{3,2,1,0:T(8,128)(2,1)S(1)}, u32[]{:S(2)}, u32[]{:S(2)}) collective-permute-start(bf16[2,2,128,512]{3,2,1,0:T(8,128)(2,1)S(1)} %get-tuple-element.55), channel_id=1, source_target_pairs={{0,2},{2,0},{1,3},{3,1},{4,6},{6,4},{5,7},{7,5},{8,10},{10,8},{9,1... | collective-permute-start | bytes 1572872 | tf_op jit(solution)/shard_map/ppermute | solution.py:288
  61.5 16.2 %collective-permute-start.19 = (bf16[2,2,128,512]{3,2,1,0:T(8,128)(2,1)S(1)}, bf16[2,2,128,512]{3,2,1,0:T(8,128)(2,1)S(1)}, u32[]{:S(2)}, u32[]{:S(2)}) collective-permute-start(bf16[2,2,128,512]{3,2,1,0:T(8,128)(2,1)S(1)} %get-tuple-element.53), channel_id=1, source_target_pairs={{0,2},{2,0},{1,3},{3,1},{4,6},{6,4},{5,7},{7,5},{8,10},{10,8},{9,1... | collective-permute-start | bytes 1572872 | tf_op jit(solution)/shard_map/ppermute | solution.py:288
  66.0 5.0 %collective-permute-start.9 = (bf16[128,512]{1,0:T(8,128)(2,1)S(1)}, bf16[128,512]{1,0:T(8,128)(2,1)S(1)}, u32[]{:S(2)}, u32[]{:S(2)}) collective-permute-start(bf16[128,512]{1,0:T(8,128)(2,1)S(1)} %get-tuple-element.82), channel_id=1, source_target_pairs={{0,4},{4,0},{1,5},{5,1},{2,6},{6,2},{3,7},{7,3},{8,12},{12,8},{9,1... | collective-permute-start | bytes 393224 | tf_op jit(solution)/shard_map/ppermute | solution.py:288
  66.6 6.2 %collective-permute-start.6 = (bf16[128,512]{1,0:T(8,128)(2,1)S(1)}, bf16[128,512]{1,0:T(8,128)(2,1)S(1)}, u32[]{:S(2)}, u32[]{:S(2)}) collective-permute-start(bf16[128,512]{1,0:T(8,128)(2,1)S(1)} %get-tuple-element.83), channel_id=1, source_target_pairs={{0,1},{1,0},{2,3},{3,2},{4,5},{5,4},{6,7},{7,6},{8,9},{9,8},{10,11... | collective-permute-start | bytes 393224 | tf_op jit(solution)/shard_map/ppermute | solution.py:288
  71.1 6.4 %collective-permute-start.10 = (bf16[2,128,512]{2,1,0:T(8,128)(2,1)S(1)}, bf16[2,128,512]{2,1,0:T(8,128)(2,1)S(1)}, u32[]{:S(2)}, u32[]{:S(2)}) collective-permute-start(bf16[2,128,512]{2,1,0:T(8,128)(2,1)S(1)} %get-tuple-element.85), channel_id=1, source_target_pairs={{0,1},{1,0},{2,3},{3,2},{4,5},{5,4},{6,7},{7,6},{8,9},{9,8},{10,11... | collective-permute-start | bytes 786440 | tf_op jit(solution)/shard_map/ppermute | solution.py:288
  72.8 6.4 %collective-permute-start.7 = (bf16[2,128,512]{2,1,0:T(8,128)(2,1)S(1)}, bf16[2,128,512]{2,1,0:T(8,128)(2,1)S(1)}, u32[]{:S(2)}, u32[]{:S(2)}) collective-permute-start(bf16[2,128,512]{2,1,0:T(8,128)(2,1)S(1)} %get-tuple-element.79), channel_id=1, source_target_pairs={{0,4},{4,0},{1,5},{5,1},{2,6},{6,2},{3,7},{7,3},{8,12},{12,8},{9,1... | collective-permute-start | bytes 786440 | tf_op jit(solution)/shard_map/ppermute | solution.py:288
  77.5 4.2 %slice-start = ((s8[8388608]{0:T(1024)(128)(4,1)}), s8[4194304]{0:T(1024)(128)(4,1)S(1)}, s32[]{:S(2)}) async-start(s8[8388608]{0:T(1024)(128)(4,1)} %bitcast.340), calls=%async_computation.7 | async-start | bytes 8388608
  77.6 2.2 collective-permute-start.11
  79.3 2.0 collective-permute-start.8
  79.8 2.3 slice-start.1
  80.3 2.8 copy-start.12
  82.1 2.2 copy-start.35
  88.5 4.8 %collective-permute-start.23 = (bf16[2,2,128,1024]{3,2,1,0:T(8,128)(2,1)}, bf16[2,2,128,1024]{3,2,1,0:T(8,128)(2,1)}, u32[]{:S(2)}, u32[]{:S(2)}) collective-permute-start(bf16[2,2,128,1024]{3,2,1,0:T(8,128)(2,1)} %bitcast.69), channel_id=1, source_target_pairs={{0,2},{2,0},{1,3},{3,1},{4,6},{6,4},{5,7},{7,5},{8,10},{10,8},{9,1... | collective-permute-start | bytes 3145736 | tf_op jit(solution)/shard_map/ppermute | solution.py:288
  91.5 6.2 %collective-permute-start.12 = (bf16[2,2,128,1024]{3,2,1,0:T(8,128)(2,1)}, bf16[2,2,128,1024]{3,2,1,0:T(8,128)(2,1)}, u32[]{:S(2)}, u32[]{:S(2)}) collective-permute-start(bf16[2,2,128,1024]{3,2,1,0:T(8,128)(2,1)} %bitcast.41), channel_id=1, source_target_pairs={{0,2},{2,0},{1,3},{3,1},{4,6},{6,4},{5,7},{7,5},{8,10},{10,8},{9,1... | collective-permute-start | bytes 3145736 | tf_op jit(solution)/shard_map/ppermute | solution.py:288
  93.2 74.1 %reduce-scatter.3.cloned.1.call-start = ((), (), s32[]{:S(2)}) async-start(), calls=%async_computation.3 | async-start | bytes 2621440 | tf_op jit(solution)/shard_map/reduce_scatter | solution.py:538
  95.3 9.2 %collective-permute-start.24 = (bf16[2,128,512]{2,1,0:T(8,128)(2,1)S(1)}, bf16[2,128,512]{2,1,0:T(8,128)(2,1)S(1)}, u32[]{:S(2)}, u32[]{:S(2)}) collective-permute-start(bf16[2,128,512]{2,1,0:T(8,128)(2,1)S(1)} %slice_bitcast_fusion.2), channel_id=1, source_target_pairs={{0,1},{1,0},{2,3},{3,2},{4,5},{5,4},{6,7},{7,6},{8,9},{9,8},{10,11... | collective-permute-start | bytes 786440 | tf_op jit(solution)/shard_map/ppermute | solution.py:288
  96.2 9.2 %collective-permute-start.26 = (bf16[2,128,512]{2,1,0:T(8,128)(2,1)S(1)}, bf16[2,128,512]{2,1,0:T(8,128)(2,1)S(1)}, u32[]{:S(2)}, u32[]{:S(2)}) collective-permute-start(bf16[2,128,512]{2,1,0:T(8,128)(2,1)S(1)} %slice_bitcast_fusion), channel_id=1, source_target_pairs={{0,4},{4,0},{1,5},{5,1},{2,6},{6,2},{3,7},{7,3},{8,12},{12,8},{9,1... | collective-permute-start | bytes 786440 | tf_op jit(solution)/shard_map/ppermute | solution.py:288
  99.3 10.8 %collective-permute-start.13 = (bf16[2,128,512]{2,1,0:T(8,128)(2,1)S(1)}, bf16[2,128,512]{2,1,0:T(8,128)(2,1)S(1)}, u32[]{:S(2)}, u32[]{:S(2)}) collective-permute-start(bf16[2,128,512]{2,1,0:T(8,128)(2,1)S(1)} %slice_bitcast_fusion.6), channel_id=1, source_target_pairs={{0,1},{1,0},{2,3},{3,2},{4,5},{5,4},{6,7},{7,6},{8,9},{9,8},{10,11... | collective-permute-start | bytes 786440 | tf_op jit(solution)/shard_map/ppermute | solution.py:288
  100.9 10.1 %collective-permute-start.15 = (bf16[2,128,512]{2,1,0:T(8,128)(2,1)S(1)}, bf16[2,128,512]{2,1,0:T(8,128)(2,1)S(1)}, u32[]{:S(2)}, u32[]{:S(2)}) collective-permute-start(bf16[2,128,512]{2,1,0:T(8,128)(2,1)S(1)} %slice_bitcast_fusion.4), channel_id=1, source_target_pairs={{0,4},{4,0},{1,5},{5,1},{2,6},{6,2},{3,7},{7,3},{8,12},{12,8},{9,1... | collective-permute-start | bytes 786440 | tf_op jit(solution)/shard_map/ppermute | solution.py:288
  105.6 8.7 %collective-permute-start.27 = (bf16[128,512]{1,0:T(8,128)(2,1)S(1)}, bf16[128,512]{1,0:T(8,128)(2,1)S(1)}, u32[]{:S(2)}, u32[]{:S(2)}) collective-permute-start(bf16[128,512]{1,0:T(8,128)(2,1)S(1)} %slice_bitcast_fusion.8), channel_id=1, source_target_pairs={{0,1},{1,0},{2,3},{3,2},{4,5},{5,4},{6,7},{7,6},{8,9},{9,8},{10,11... | collective-permute-start | bytes 393224 | tf_op jit(solution)/shard_map/ppermute | solution.py:288
  106.9 7.4 %collective-permute-start.25 = (bf16[128,512]{1,0:T(8,128)(2,1)S(1)}, bf16[128,512]{1,0:T(8,128)(2,1)S(1)}, u32[]{:S(2)}, u32[]{:S(2)}) collective-permute-start(bf16[128,512]{1,0:T(8,128)(2,1)S(1)} %slice_bitcast_fusion.10), channel_id=1, source_target_pairs={{0,4},{4,0},{1,5},{5,1},{2,6},{6,2},{3,7},{7,3},{8,12},{12,8},{9,1... | collective-permute-start | bytes 393224 | tf_op jit(solution)/shard_map/ppermute | solution.py:288
  111.2 6.4 %copy-start.4 = (bf16[128,1024]{1,0:T(8,128)(2,1)S(1)}, bf16[128,1024]{1,0:T(8,128)(2,1)}, u32[]{:S(2)}) copy-start(bf16[128,1024]{1,0:T(8,128)(2,1)} %param.17) | copy-start | bytes 786436
  111.2 5.0 %collective-permute-start.16 = (bf16[128,512]{1,0:T(8,128)(2,1)S(1)}, bf16[128,512]{1,0:T(8,128)(2,1)S(1)}, u32[]{:S(2)}, u32[]{:S(2)}) collective-permute-start(bf16[128,512]{1,0:T(8,128)(2,1)S(1)} %slice_bitcast_fusion.12), channel_id=1, source_target_pairs={{0,1},{1,0},{2,3},{3,2},{4,5},{5,4},{6,7},{7,6},{8,9},{9,8},{10,11... | collective-permute-start | bytes 393224 | tf_op jit(solution)/shard_map/ppermute | solution.py:288
  112.5 5.0 %collective-permute-start.14 = (bf16[128,512]{1,0:T(8,128)(2,1)S(1)}, bf16[128,512]{1,0:T(8,128)(2,1)S(1)}, u32[]{:S(2)}, u32[]{:S(2)}) collective-permute-start(bf16[128,512]{1,0:T(8,128)(2,1)S(1)} %slice_bitcast_fusion.14), channel_id=1, source_target_pairs={{0,4},{4,0},{1,5},{5,1},{2,6},{6,2},{3,7},{7,3},{8,12},{12,8},{9,1... | collective-permute-start | bytes 393224 | tf_op jit(solution)/shard_map/ppermute | solution.py:288
  116.3 3.4 copy-start.13
  116.3 3.4 copy-start.15
  116.3 3.4 copy-start.37
  116.3 3.4 copy-start.39
  118.8 6.9 %collective-permute-start.28 = (bf16[144,1024]{1,0:T(8,128)(2,1)S(1)}, bf16[144,1024]{1,0:T(8,128)(2,1)}, u32[]{:S(2)}, u32[]{:S(2)}) collective-permute-start(bf16[144,1024]{1,0:T(8,128)(2,1)S(1)} %fusion.50), channel_id=1, source_target_pairs={{0,1},{1,0},{2,3},{3,2},{4,5},{5,4},{6,7},{7,6},{8,9},{9,8},{10,11... | collective-permute-start | bytes 884744 | tf_op jit(solution)/shard_map/ppermute | solution.py:288
  122.4 6.7 %copy-start.23 = (bf16[2,128,4,64]{1,0,3,2:T(2,128)(2,1)S(1)}, bf16[2,128,4,64]{1,0,3,2:T(2,128)(2,1)}, u32[]{:S(2)}) copy-start(bf16[2,128,4,64]{1,0,3,2:T(2,128)(2,1)} %reshape.244) | copy-start | bytes 393220
  122.4 6.7 %copy-start.31 = (f32[2,4,2,128]{3,2,1,0:T(2,128)S(1)}, f32[2,4,2,128]{3,2,1,0:T(2,128)}, u32[]{:S(2)}) copy-start(f32[2,4,2,128]{3,2,1,0:T(2,128)} %copy-done.30) | copy-start | bytes 24580
  122.4 139.4 %all-reduce.5.cloned.1.call-start = ((), (), s32[]{:S(2)}) async-start(), calls=%async_computation.2 | async-start | bytes 6488064 | tf_op jit(solution)/shard_map/psum | solution.py:555
  136.5 10.5 %collective-permute-start.29 = (bf16[256,1024]{0,1:T(8,128)(2,1)S(1)}, bf16[256,1024]{0,1:T(8,128)(2,1)S(1)}, u32[]{:S(2)}, u32[]{:S(2)}) collective-permute-start(bf16[256,1024]{0,1:T(8,128)(2,1)S(1)} %fusion.36), channel_id=1, source_target_pairs={{0,1},{1,0},{2,3},{3,2},{4,5},{5,4},{6,7},{7,6},{8,9},{9,8},{10,11... | collective-permute-start | bytes 1572872 | tf_op jit(solution)/shard_map/ppermute | solution.py:288
  137.9 9.1 %copy-start.8 = (bf16[512,512]{1,0:T(8,128)(2,1)S(1)}, bf16[512,512]{1,0:T(8,128)(2,1)}, u32[]{:S(2)}) copy-start(bf16[512,512]{1,0:T(8,128)(2,1)} %param.21) | copy-start | bytes 1572868
  138.4 9.0 %copy-start.10 = (bf16[512,512]{1,0:T(8,128)(2,1)S(1)}, bf16[512,512]{1,0:T(8,128)(2,1)}, u32[]{:S(2)}) copy-start(bf16[512,512]{1,0:T(8,128)(2,1)} %param.20) | copy-start | bytes 1572868
  152.8 19.8 %copy-start.3 = (f32[128,1024]{1,0:T(8,128)S(1)}, f32[128,1024]{1,0:T(8,128)}, u32[]{:S(2)}) copy-start(f32[128,1024]{1,0:T(8,128)} %get-tuple-element.19) | copy-start | bytes 1572868
  152.8 19.8 %copy-start.33 = (f32[128]{0:T(128)S(1)}, f32[128]{0:T(128)}, u32[]{:S(2)}) copy-start(f32[128]{0:T(128)} %copy-done.32) | copy-start | bytes 1540
  152.8 19.8 %copy-start.34 = (f32[128]{0:T(128)S(1)}, f32[128]{0:T(128)}, u32[]{:S(2)}) copy-start(f32[128]{0:T(128)} %get-tuple-element.16) | copy-start | bytes 1540
  152.8 160.3 %all-gather.5.cloned.1.call-start = ((), (), s32[]{:S(2)}) async-start(), calls=%async_computation.6 | async-start | bytes 4456448 | tf_op jit(solution)/shard_map/all_gather | solution.py:539
  153.4 234.4 %all-gather.3.cloned.1.call-start = ((), (), s32[]{:S(2)}) async-start(), calls=%async_computation.4 | async-start | bytes 8912896 | tf_op jit(solution)/shard_map/all_gather | solution.py:539
  167.4 5.0 %collective-permute-start.30 = (bf16[128,512]{1,0:T(8,128)(2,1)S(1)}, bf16[128,512]{1,0:T(8,128)(2,1)S(1)}, u32[]{:S(2)}, u32[]{:S(2)}) collective-permute-start(bf16[128,512]{1,0:T(8,128)(2,1)S(1)} %slice.411), channel_id=1, source_target_pairs={{0,1},{1,0},{2,3},{3,2},{4,5},{5,4},{6,7},{7,6},{8,9},{9,8},{10,11... | collective-permute-start | bytes 393224 | tf_op jit(solution)/shard_map/ppermute | solution.py:288
  263.1 3.0 copy-start.1
  (14 other events, 16.7 us)
Sparse Core Ops, SparseCore 0:
  93.4 27.9 reduce-scatter.4
  124.2 43.0 reduce-scatter.2
Sparse Core Ops, SparseCore 1:
  152.9 108.8 all-reduce.4
  263.9 49.2 all-gather.4
  315.2 72.6 all-gather.2
